TPU v7x, 128 devices: a whole 4x4x4 slice. The times are simulated.
128 devices in a mesh: aux: 16 (over z, x_lo, core), rows: 8 (over y, x_hi).
Axes of the slice: x: 4 (x_hi: 2, x_lo: 2; x = x_hi * 2 + x_lo), y: 4, z: 4, core: 2. Of those that a mesh axis runs over, the one named last changes fastest.
Arguments:
- three_center: bfloat16 [128, 40, 16, 128, 128], P('aux', 'rows'), may hold values from -6 to 6
- coeffs: bfloat16 [16384, 128], P('aux'), may hold values from -0.01171875 to 0.01171875
- sig_blocks: int32 [40, 16], P('rows'), may hold values from 0 to 7
- k_columns: int32 [40, 12], P('rows'), may hold values from 0 to 39, as said below
- owners: int32 [480, 1], P('rows'), may hold values from 0 to 7; in each aligned block of 60 rows (0 to 59, 60 to 119, ...) at most 15 rows name the same one
Outputs:
- exchange_blocks: float32 [960, 128, 128], P('rows', 'aux')
Inputs may be any that keep to these rules, and one draw needn't show every extreme that they name: `owners`: among the 60 entries of one rows index, no owner is named more than 15 times. `k_columns`: the 12 entries of one row block are distinct, and the first entry of row block m is m itself.
All inputs are finite; a program needn't handle non-finite values.
Results may differ from a plain program's by a relative error of at most 0.0014.
Values may be sent and summed in bfloat16 or wider, within the bound.
A program may use at most 128 MiB of HBM per device.

v0:
```python
import jax
import jax.numpy as jnp
from jax import lax
from jax.sharding import PartitionSpec as P

BS = 128
OCC = 128
BLK_DEV = 8
CAP = 15


def bucket(values, owner_ids, owner_total, capacity):
    onehot = (owner_ids[:, None] == jnp.arange(owner_total, dtype=jnp.int32)[None, :]).astype(
        jnp.int32
    )
    ranks = jnp.sum(jnp.cumsum(onehot, axis=0) * onehot, axis=1) - 1
    target = owner_ids * capacity + ranks
    buffer = jnp.zeros((owner_total * capacity,) + values.shape[1:], values.dtype)
    return buffer.at[target].set(values)


def per_device(three_center, coeffs, sig_blocks, k_columns, owners):
    row_local = three_center.shape[1]
    owner_count = three_center.shape[2]
    panels = lax.all_gather(coeffs, "aux", axis=0, tiled=True)
    blocks = panels.reshape(owner_count * BLK_DEV, BS, OCC)
    wanted = sig_blocks + (jnp.arange(owner_count, dtype=jnp.int32) * BLK_DEV)[None, :]
    picked = blocks[wanted]
    half_sum = jnp.einsum(
        "pmqab,mqbo->pmao", three_center, picked, preferred_element_type=jnp.float32
    )
    half = half_sum.astype(jnp.bfloat16)
    every_row = lax.all_gather(half, "rows", axis=1, tiled=True)
    pieces_list = []
    for index in range(row_local):
        partners = jnp.take(every_row, k_columns[index], axis=1)
        pieces_list.append(
            jnp.einsum(
                "pai,psbi->sab", half[:, index], partners, preferred_element_type=jnp.float32
            )
        )
    partial_value = jnp.concatenate(pieces_list, axis=0)
    owner_total = lax.axis_size("rows")
    owner_ids = owners[:, 0]
    reduced = lax.psum_scatter(partial_value, "aux", scatter_dimension=1, tiled=True)
    buffer = bucket(reduced, owner_ids, owner_total, CAP)
    buffer = buffer.reshape(owner_total, CAP, reduced.shape[1], BS)
    arrived = lax.all_to_all(buffer, "rows", split_axis=0, concat_axis=0, tiled=True)
    return arrived.reshape(owner_total * CAP, reduced.shape[1], BS)


def solution(mesh):
    return jax.shard_map(
        per_device,
        mesh=mesh,
        in_specs=(
            P("aux", "rows", None, None, None),
            P("aux", None),
            P("rows", None),
            P("rows", None),
            P("rows", None),
        ),
        out_specs=P("rows", "aux", None),
        check_vma=False,
    )
```

profile of v0, /device:TPU:0, one launch (start us, length us, event | category | flops | bytes accessed | tf_op | source)
XLA Modules:
  0.0 333.1 jit_solution(17910618142357279781)
XLA Ops:
  6.5 0.7 all-gather.3.cloned.1.call-update
  7.3 0.0 all-gather.5.cloned.1.call-start
  7.3 0.7 compare_select_fusion
  8.0 0.1 reshape.72
  8.1 40.8 %all-gather.3.cloned.1.call-done = bf16[16384,128]{1,0:T(8,128)(2,1)} async-done(((bf16[1024,128]{1,0:T(8,128)(2,1)}), bf16[16384,128]{1,0:T(8,128)(2,1)}) %all-gather.3.cloned.1.call-update) | async-done | bytes 4194320 | tf_op jit(solution)/shard_map/all_gather | solution.py:25
  48.9 3.2 gather_fusion
  52.1 12.0 %fusion.29 = bf16[8,5,128,128]{2,3,0,1:T(8,128)(2,1)} fusion(bf16[5,16,128,128,1]{3,2,1,4,0:T(8,128)(2,1)S(1)} %bitcast.135, bf16[8,5,16,128,128]{4,3,2,1,0:T(8,128)(2,1)} %param.7), kind=kOutput, calls=%fused_computation.35 | convolution fusion | flops 2685009920 | bytes 24903680 | tf_op jit(solution)/shard_map/pmqab,mqbo->pmao/dot_general | solution.py:29
  64.1 2.4 copy.33
  66.6 0.0 all-gather.5.cloned.1.call-update
  66.6 0.0 reduce-scatter.2.cloned.1.call-start
  66.7 125.3 %all-gather.5.cloned.1.call-done = bf16[8,40,128,128]{3,2,0,1:T(8,128)(2,1)} async-done(((bf16[8,5,128,128]{3,2,0,1:T(8,128)(2,1)}), bf16[8,40,128,128]{3,2,0,1:T(8,128)(2,1)}) %all-gather.5.cloned.1.call-update) | async-done | bytes 10485776 | tf_op jit(solution)/shard_map/all_gather | solution.py:33
  192.0 5.1 %gather_fusion.1 = bf16[12,8,128,128]{3,2,1,0:T(8,128)(2,1)S(1)} fusion(bf16[8,40,128,128]{3,2,0,1:T(8,128)(2,1)} %all-gather.5.cloned.1.call-done, s32[1024]{0:T(1024)S(1)} %pad_clamp_fusion.4), kind=kCustom, calls=%fused_computation.clone | custom fusion | bytes 6291504 | tf_op jit(solution)/shard_map/jit(_take)/gather | solution.py:36
  197.2 2.9 fusion.35
  200.0 5.1 %gather_fusion.2 = bf16[12,8,128,128]{3,2,1,0:T(8,128)(2,1)S(1)} fusion(bf16[8,40,128,128]{3,2,0,1:T(8,128)(2,1)} %all-gather.5.cloned.1.call-done, s32[1024]{0:T(1024)S(1)} %get-tuple-element.27), kind=kCustom, calls=%fused_computation.1.clone | custom fusion | bytes 6291504 | tf_op jit(solution)/shard_map/jit(_take)/gather | solution.py:36
  205.2 2.8 fusion.41
  208.0 5.1 %gather_fusion.3 = bf16[12,8,128,128]{3,2,1,0:T(8,128)(2,1)S(1)} fusion(bf16[8,40,128,128]{3,2,0,1:T(8,128)(2,1)} %all-gather.5.cloned.1.call-done, s32[1024]{0:T(1024)S(1)} %get-tuple-element.26), kind=kCustom, calls=%fused_computation.2.clone | custom fusion | bytes 6291504 | tf_op jit(solution)/shard_map/jit(_take)/gather | solution.py:36
  213.1 2.9 fusion.47
  216.0 5.1 %gather_fusion.4 = bf16[12,8,128,128]{3,2,1,0:T(8,128)(2,1)S(1)} fusion(bf16[8,40,128,128]{3,2,0,1:T(8,128)(2,1)} %all-gather.5.cloned.1.call-done, s32[1024]{0:T(1024)S(1)} %get-tuple-element.25), kind=kCustom, calls=%fused_computation.3.clone | custom fusion | bytes 6291504 | tf_op jit(solution)/shard_map/jit(_take)/gather | solution.py:36
  221.1 2.9 fusion.53
  224.1 5.1 %gather_fusion.5 = bf16[12,8,128,128]{3,2,1,0:T(8,128)(2,1)S(1)} fusion(bf16[8,40,128,128]{3,2,0,1:T(8,128)(2,1)} %all-gather.5.cloned.1.call-done, s32[1024]{0:T(1024)S(1)} %get-tuple-element.24), kind=kCustom, calls=%fused_computation.4.clone | custom fusion | bytes 6291504 | tf_op jit(solution)/shard_map/jit(_take)/gather | solution.py:36
  229.2 2.9 fusion.59
  232.1 5.1 %copy.39 = f32[60,128,128]{2,0,1:T(8,128)} copy(f32[60,128,128]{1,2,0:T(8,128)} %fusion.59) | data formatting | bytes 7864320 | tf_op jit(solution)/shard_map/concatenate | solution.py:42
  237.2 0.0 reduce-scatter.2.cloned.1.call-update
  237.2 0.6 copy-done
  237.8 0.1 fusion.62
  237.9 0.1 reduce_window_sum.11
  238.0 0.2 select_reduce_fusion
  238.2 67.7 %reduce-scatter.2.cloned.1.call-done = f32[60,8,128]{2,0,1:T(8,128)} async-done(((f32[60,128,128]{2,0,1:T(8,128)}), f32[60,8,128]{2,0,1:T(8,128)}) %reduce-scatter.2.cloned.1.call-update) | async-done | bytes 245776 | tf_op jit(solution)/shard_map/reduce_scatter | solution.py:45
  305.9 1.1 copy.40
  307.1 2.5 scatter_fusion
  309.6 16.2 %all_to_all.5 = f32[8,15,8,128]{3,2,1,0:T(8,128)S(1)} all-to-all(f32[8,15,8,128]{3,2,1,0:T(8,128)S(1)} %bitcast.134), channel_id=1, replica_groups=mesh['aux'=16,'rows'=8] {'rows'}, dimensions={0} | all-to-all | bytes 983040 | tf_op jit(solution)/shard_map/all_to_all | solution.py:48
  325.8 0.8 copy.70
  (12 shorter events, 0.1 us)
Async XLA Ops:
  6.5 42.4 %all-gather.3.cloned.1.call-start = ((), (), s32[]{:S(2)}) async-start(), calls=%async_computation.2 | async-start | bytes 4456448 | tf_op jit(solution)/shard_map/all_gather | solution.py:25
  7.3 184.8 %all-gather.5.cloned.1.call-start = ((), (), s32[]{:S(2)}) async-start(), calls=%async_computation.3 | async-start | bytes 11796480 | tf_op jit(solution)/shard_map/all_gather | solution.py:33
  64.1 2.5 copy-start.1
  66.6 239.3 %reduce-scatter.2.cloned.1.call-start = ((), (), s32[]{:S(2)}) async-start(), calls=%async_computation.4 | async-start | bytes 4456448 | tf_op jit(solution)/shard_map/reduce_scatter | solution.py:45
  237.2 0.7 copy-start
Sparse Core Ops, SparseCore 0:
  9.0 39.8 all-gather.2
  66.7 125.2 all-gather.4
  237.3 68.5 reduce-scatter.1
where the time goes:
time: 334 us; the launch traced here: 333 us
  waiting for transfers between devices  235 us (70%)
  local copies, waits for them, and re-layouts  41.5 us (12%)
  matrix products  26.4 us (8%)
  blocking collectives  16.2 us (5%)
  between operations  13.2 us (4%)
    all_gather x1, waiting for transfers between devices, per_device(): every_row = lax.all_gather(half, 'rows', axis=1, tiled=True)  125 us
    reduce_scatter x1, waiting for transfers between devices, per_device(): lax.psum_scatter(partial_value, 'aux', scatter_dimension=1, tiled=True)  67.7 us
    all_gather x1, waiting for transfers between devices, per_device(): panels = lax.all_gather(coeffs, 'aux', axis=0, tiled=True)  40.8 us
    gather x5, local copies, waits for them, and re-layouts, per_device(): partners = jnp.take(every_row, k_columns[index], axis=1)  25.6 us
    all_to_all x1, blocking collectives, per_device(): lax.all_to_all(buffer, 'rows', split_axis=0, concat_axis=0, tiled=True)  16.2 us
    dot_general x5, matrix products, per_device(): jnp.einsum('pai,psbi->sab', half[:, index], partners, preferred_element_t...  14.4 us
    dot_general x1, matrix products, per_device(): jnp.einsum('pmqab,mqbo->pmao', three_center, picked, preferred_element_ty...  12 us
  transfers between devices with their start and end apart: 3, of which 3 were waited for; matrix products, arithmetic and copies ran while one was open for 0% of the time, Pallas kernels for 0%

commit v1 on v0

--- a/solution.py
+++ b/solution.py
@@ -22,7 +22,9 @@
 def per_device(three_center, coeffs, sig_blocks, k_columns, owners):
     row_local = three_center.shape[1]
     owner_count = three_center.shape[2]
-    panels = lax.all_gather(coeffs, "aux", axis=0, tiled=True)
+    panels = jnp.concatenate(
+        lax.all_to_all(jnp.stack([coeffs] * lax.axis_size("aux")), "aux", 0, 0), axis=0
+    )
     blocks = panels.reshape(owner_count * BLK_DEV, BS, OCC)
     wanted = sig_blocks + (jnp.arange(owner_count, dtype=jnp.int32) * BLK_DEV)[None, :]
     picked = blocks[wanted]

time: 334 us -> 352 us (1.054)
  waiting for transfers between devices: 235 us -> 243 us
  starting transfers between devices: 0.08 us -> 6.9 us
  local copies, waits for them, and re-layouts: 41.5 us -> 45.3 us
    all_to_all x0 -> x1, waiting for transfers between devices: none -> 50.2 us  [per_device(): lax.all_to_all(jnp.stack([coeffs] * lax.axis_size('aux')), 'aux', 0, 0)]
    all_gather x1 -> x0, waiting for transfers between devices: 40.8 us -> none  [per_device(): panels = lax.all_gather(coeffs, 'aux', axis=0, tiled=True)]
    all_to_all x0 -> x1, starting transfers between devices: none -> 6.64 us  [per_device(): lax.all_to_all(jnp.stack([coeffs] * lax.axis_size('aux')), 'aux', 0, 0)]
    another operation x0 -> x1, local copies, waits for them, and re-layouts: none -> 3.73 us  [per_device(): jnp.stack([coeffs] * lax.axis_size('aux'))]
where the time goes in v1:
time: 352 us; the launch traced here: 351 us
  waiting for transfers between devices  243 us (69%)
  local copies, waits for them, and re-layouts  45.3 us (13%)
  matrix products  26.3 us (7%)
  blocking collectives  16.2 us (5%)
  between operations  13.6 us (4%)
  starting transfers between devices  6.9 us (2%)
    all_gather x1, waiting for transfers between devices, per_device(): every_row = lax.all_gather(half, 'rows', axis=1, tiled=True)  125 us
    reduce_scatter x1, waiting for transfers between devices, per_device(): lax.psum_scatter(partial_value, 'aux', scatter_dimension=1, tiled=True)  67.7 us
    all_to_all x1, waiting for transfers between devices, per_device(): lax.all_to_all(jnp.stack([coeffs] * lax.axis_size('aux')), 'aux', 0, 0)  50.2 us
    gather x5, local copies, waits for them, and re-layouts, per_device(): partners = jnp.take(every_row, k_columns[index], axis=1)  25.6 us
    all_to_all x1, blocking collectives, per_device(): lax.all_to_all(buffer, 'rows', split_axis=0, concat_axis=0, tiled=True)  16.2 us
    dot_general x5, matrix products, per_device(): jnp.einsum('pai,psbi->sab', half[:, index], partners, preferred_element_t...  14.3 us
    dot_general x1, matrix products, per_device(): jnp.einsum('pmqab,mqbo->pmao', three_center, picked, preferred_element_ty...  12 us
  transfers between devices with their start and end apart: 3, of which 3 were waited for; matrix products, arithmetic and copies ran while one was open for 0% of the time, Pallas kernels for 0%

profile of v1, /device:TPU:0, one launch (start us, length us, event | category | flops | bytes accessed | tf_op | source)
XLA Modules:
  0.0 351.3 jit_solution(7077086093806445569)
XLA Ops:
  6.5 3.7 %stack.2 = bf16[16,1024,128]{2,1,0:T(8,128)(2,1)} broadcast(bf16[1024,128]{1,0:T(8,128)(2,1)} %param.8), dimensions={1,2} | broadcast | bytes 4456448 | tf_op jit(solution)/shard_map/stack | solution.py:26
  10.3 6.6 %all-to-all-start = ((bf16[16,1024,128]{2,1,0:T(8,128)(2,1)}), bf16[16,1024,128]{2,1,0:T(8,128)(2,1)}, u32[]{:S(2)}, u32[]{:S(2)}) async-start(bf16[16,1024,128]{2,1,0:T(8,128)(2,1)} %stack.2), calls=%async_computation | async-start | bytes 8388608 | tf_op jit(solution)/shard_map/all_to_all | solution.py:26
  16.9 0.0 all-gather.2.cloned.1.call-start
  17.0 0.1 reshape.70
  17.1 50.2 %all-to-all-done = bf16[16,1024,128]{2,1,0:T(8,128)(2,1)} async-done(((bf16[16,1024,128]{2,1,0:T(8,128)(2,1)}), bf16[16,1024,128]{2,1,0:T(8,128)(2,1)}, u32[]{:S(2)}, u32[]{:S(2)}) %all-to-all-start) | async-done | bytes 4194336 | tf_op jit(solution)/shard_map/all_to_all | solution.py:26
  67.2 3.2 gather_fusion
  70.5 12.0 %fusion.29 = bf16[8,5,128,128]{2,3,0,1:T(8,128)(2,1)} fusion(bf16[5,16,128,128,1]{3,2,1,4,0:T(8,128)(2,1)S(1)} %bitcast.134, bf16[8,5,16,128,128]{4,3,2,1,0:T(8,128)(2,1)} %param.7), kind=kOutput, calls=%fused_computation.35 | convolution fusion | flops 2685009920 | bytes 24903680 | tf_op jit(solution)/shard_map/pmqab,mqbo->pmao/dot_general | solution.py:31
  82.5 2.4 copy.32
  84.9 0.0 all-gather.2.cloned.1.call-update
  85.0 0.2 reduce-scatter.2.cloned.1.call-start
  85.3 124.8 %all-gather.2.cloned.1.call-done = bf16[8,40,128,128]{3,2,0,1:T(8,128)(2,1)} async-done(((bf16[8,5,128,128]{3,2,0,1:T(8,128)(2,1)}), bf16[8,40,128,128]{3,2,0,1:T(8,128)(2,1)}) %all-gather.2.cloned.1.call-update) | async-done | bytes 10485776 | tf_op jit(solution)/shard_map/all_gather | solution.py:35
  210.1 5.1 %gather_fusion.1 = bf16[12,8,128,128]{3,2,1,0:T(8,128)(2,1)S(1)} fusion(bf16[8,40,128,128]{3,2,0,1:T(8,128)(2,1)} %all-gather.2.cloned.1.call-done, s32[1024]{0:T(1024)S(1)} %pad_clamp_fusion.4), kind=kCustom, calls=%fused_computation.clone | custom fusion | bytes 6291504 | tf_op jit(solution)/shard_map/jit(_take)/gather | solution.py:38
  215.2 2.8 fusion.35
  218.0 5.1 %gather_fusion.2 = bf16[12,8,128,128]{3,2,1,0:T(8,128)(2,1)S(1)} fusion(bf16[8,40,128,128]{3,2,0,1:T(8,128)(2,1)} %all-gather.2.cloned.1.call-done, s32[1024]{0:T(1024)S(1)} %get-tuple-element.27), kind=kCustom, calls=%fused_computation.1.clone | custom fusion | bytes 6291504 | tf_op jit(solution)/shard_map/jit(_take)/gather | solution.py:38
  223.2 2.8 fusion.41
  226.0 5.1 %gather_fusion.3 = bf16[12,8,128,128]{3,2,1,0:T(8,128)(2,1)S(1)} fusion(bf16[8,40,128,128]{3,2,0,1:T(8,128)(2,1)} %all-gather.2.cloned.1.call-done, s32[1024]{0:T(1024)S(1)} %get-tuple-element.26), kind=kCustom, calls=%fused_computation.2.clone | custom fusion | bytes 6291504 | tf_op jit(solution)/shard_map/jit(_take)/gather | solution.py:38
  231.2 2.9 fusion.47
  234.0 5.1 %gather_fusion.4 = bf16[12,8,128,128]{3,2,1,0:T(8,128)(2,1)S(1)} fusion(bf16[8,40,128,128]{3,2,0,1:T(8,128)(2,1)} %all-gather.2.cloned.1.call-done, s32[1024]{0:T(1024)S(1)} %get-tuple-element.25), kind=kCustom, calls=%fused_computation.3.clone | custom fusion | bytes 6291504 | tf_op jit(solution)/shard_map/jit(_take)/gather | solution.py:38
  239.2 2.9 fusion.53
  242.1 5.1 %gather_fusion.5 = bf16[12,8,128,128]{3,2,1,0:T(8,128)(2,1)S(1)} fusion(bf16[8,40,128,128]{3,2,0,1:T(8,128)(2,1)} %all-gather.2.cloned.1.call-done, s32[1024]{0:T(1024)S(1)} %get-tuple-element.24), kind=kCustom, calls=%fused_computation.4.clone | custom fusion | bytes 6291504 | tf_op jit(solution)/shard_map/jit(_take)/gather | solution.py:38
  247.2 2.9 fusion.59
  250.1 5.1 %copy.38 = f32[60,128,128]{2,0,1:T(8,128)} copy(f32[60,128,128]{1,2,0:T(8,128)} %fusion.59) | data formatting | bytes 7864320 | tf_op jit(solution)/shard_map/concatenate | solution.py:44
  255.2 0.0 reduce-scatter.2.cloned.1.call-update
  255.2 0.6 copy-done.1
  255.9 0.1 fusion.62
  255.9 0.1 reduce_window_sum.11
  256.0 0.2 select_reduce_fusion
  256.2 67.7 %reduce-scatter.2.cloned.1.call-done = f32[60,8,128]{2,0,1:T(8,128)} async-done(((f32[60,128,128]{2,0,1:T(8,128)}), f32[60,8,128]{2,0,1:T(8,128)}) %reduce-scatter.2.cloned.1.call-update) | async-done | bytes 245776 | tf_op jit(solution)/shard_map/reduce_scatter | solution.py:47
  323.9 1.1 copy.39
  325.0 2.5 scatter_fusion
  327.5 16.2 %all_to_all.10 = f32[8,15,8,128]{3,2,1,0:T(8,128)S(1)} all-to-all(f32[8,15,8,128]{3,2,1,0:T(8,128)S(1)} %bitcast.133), channel_id=1, replica_groups=mesh['aux'=16,'rows'=8] {'rows'}, dimensions={0} | all-to-all | bytes 983040 | tf_op jit(solution)/shard_map/all_to_all | solution.py:50
  343.7 0.8 copy.71
  (14 shorter events, 0.1 us)
Async XLA Ops:
  10.3 6.7 %copy-start = (s32[5,16]{1,0:T(8,128)S(1)}, s32[5,16]{1,0:T(8,128)}, u32[]{:S(2)}) copy-start(s32[5,16]{1,0:T(8,128)} %param.9) | copy-start | bytes 964
  10.3 57.0 %all-to-all-start = ((bf16[16,1024,128]{2,1,0:T(8,128)(2,1)}), bf16[16,1024,128]{2,1,0:T(8,128)(2,1)}, u32[]{:S(2)}, u32[]{:S(2)}) async-start(bf16[16,1024,128]{2,1,0:T(8,128)(2,1)} %stack.2), calls=%async_computation | async-start | bytes 8388608 | tf_op jit(solution)/shard_map/all_to_all | solution.py:26
  16.9 193.1 %all-gather.2.cloned.1.call-start = ((), (), s32[]{:S(2)}) async-start(), calls=%async_computation.3 | async-start | bytes 11796480 | tf_op jit(solution)/shard_map/all_gather | solution.py:35
  82.5 2.7 copy-start.2
  85.0 238.9 %reduce-scatter.2.cloned.1.call-start = ((), (), s32[]{:S(2)}) async-start(), calls=%async_computation.4 | async-start | bytes 4456448 | tf_op jit(solution)/shard_map/reduce_scatter | solution.py:47
  255.2 0.7 copy-start.1
Sparse Core Ops, SparseCore 0:
  85.1 124.9 all-gather.1
  255.3 68.5 reduce-scatter.1
